TPU v7x, 128 devices: a whole 4x4x4 slice. The times are simulated.
128 devices in a mesh: row: 8 (over y, core), col: 16 (over z, x).
Axes of the slice: x: 4, y: 4, z: 4, core: 2. Of those that a mesh axis runs over, the one named last changes fastest.
Arguments:
- amplitudes: bfloat16 [16, 16, 4, 128, 128], P('row', 'col'), may hold values from -6 to 6
- cholesky: bfloat16 [16, 16, 10, 128, 128], P('row', 'col'), may hold values from -0.5 to 0.5, as said below
- tile_mask: int32 [16, 16], P('row', 'col'), may hold values 0 or 1
Outputs:
- antisymmetrized: bfloat16 [16, 16, 4, 128, 128], P('row', 'col')
Inputs may be any that keep to these rules, and one draw needn't show every extreme that they name: cholesky is symmetric: cholesky[a,c,q,x,u] equals cholesky[c,a,q,u,x].
All inputs are finite; a program needn't handle non-finite values. No bound on the sum of `tile_mask` on one device may be relied on, other than what follows from the above.
Results may differ from a plain program's by a relative error of at most 0.0059.
Values may be sent and summed in bfloat16 or wider, within the bound.
A program may use at most 128 MiB of HBM per device.

v0:
```python
import math
import jax
import jax.numpy as jnp
from jax import lax
from jax.sharding import PartitionSpec as P


def from_partner(value, axis, apart):
    mask = 2**apart
    pairs = [(source, source ^ mask) for source in range(lax.axis_size(axis))]
    return lax.ppermute(value, axis, pairs)


def flip_row(tile_set, bit_pos):
    bit_value = lax.axis_index("row") >> bit_pos & 1
    kept = lax.dynamic_index_in_dim(tile_set, bit_value, 0, keepdims=False)
    outgoing = lax.dynamic_index_in_dim(tile_set, 1 - bit_value, 0, keepdims=False)
    incoming = from_partner(outgoing, "row", bit_pos)
    slot_zero = jnp.where(bit_value == 0, kept, incoming)
    slot_one = jnp.where(bit_value == 0, incoming, kept)
    return jnp.stack([slot_zero, slot_one])


def flip_col(tile_set, bit_pos):
    bit_value = lax.axis_index("col") >> bit_pos & 1
    kept = lax.dynamic_index_in_dim(tile_set, bit_value, 0, keepdims=False)
    outgoing = lax.dynamic_index_in_dim(tile_set, 1 - bit_value, 0, keepdims=False)
    incoming = from_partner(outgoing, "col", bit_pos)
    slot_zero = jnp.where(bit_value == 0, kept, incoming)
    slot_one = jnp.where(bit_value == 0, incoming, kept)
    return jnp.stack([slot_zero, slot_one])


def mirror_cascade(tile_set):
    col_bits = lax.axis_size("col").bit_length() - 1
    tile_set = flip_col(tile_set, 0)
    for bit_pos in range(1, col_bits):
        tile_set = flip_row(tile_set, bit_pos - 1)
        tile_set = flip_col(tile_set, bit_pos)
        tile_set = flip_row(tile_set, bit_pos - 1)
    return tile_set


def body(amplitudes, cholesky, tile_mask):
    tile_rows = amplitudes.shape[0]
    pair_count = amplitudes.shape[2]
    tile_edge = amplitudes.shape[3]
    vectors = cholesky.shape[2]
    occupied = math.isqrt(pair_count)
    column = lax.all_gather(cholesky, "row", axis=0, tiled=True)
    column_mats = jnp.transpose(column[:, 0], (0, 2, 1, 3)).reshape(
        column.shape[0], tile_edge, vectors * tile_edge
    )
    amp_block = lax.all_gather(amplitudes, "col", axis=1, tiled=True)
    mask_block = lax.all_gather(tile_mask, "col", axis=1, tiled=True)
    tile_count = amp_block.shape[1]
    masked = amp_block * mask_block.astype(jnp.bfloat16)[:, :, None, None, None]
    masked = masked.reshape(amp_block.shape[0], tile_count, pair_count * tile_edge, tile_edge)
    halves = jnp.einsum("cnmv,nvz->cmz", masked, column_mats, preferred_element_type=jnp.float32)
    halves = halves.astype(jnp.bfloat16).reshape(
        tile_rows, pair_count, tile_edge, vectors, tile_edge
    )
    spread = lax.all_gather(cholesky, "col", axis=1, tiled=True)
    ladder = lax.psum_scatter(
        jnp.einsum("caqux,cpuqy->apxy", spread, halves, preferred_element_type=jnp.float32),
        "row",
        scatter_dimension=0,
        tiled=True,
    )
    rounded = ladder.astype(jnp.bfloat16)
    mirror = mirror_cascade(rounded)
    own_tiles = lax.optimization_barrier(rounded).astype(jnp.float32)
    flipped = mirror.reshape(tile_rows, occupied, occupied, tile_edge, tile_edge)
    flipped = jnp.transpose(flipped, (0, 2, 1, 4, 3)).reshape(
        tile_rows, pair_count, tile_edge, tile_edge
    )
    result_tiles = (own_tiles - flipped.astype(jnp.float32)).astype(jnp.bfloat16)
    return result_tiles.reshape(tile_rows, 1, pair_count, tile_edge, tile_edge)


def solution(mesh):
    in_specs = (
        P("row", "col", None, None, None),
        P("row", "col", None, None, None),
        P("row", "col"),
    )
    out_specs = P("row", "col", None, None, None)
    return jax.shard_map(body, mesh=mesh, in_specs=in_specs, out_specs=out_specs, check_vma=False)
```

profile of v0, /device:TPU:0, one launch (start us, length us, event | category | flops | bytes accessed | tf_op | source)
XLA Modules:
  0.0 314.2 jit_solution(16139904179975113621)
XLA Ops:
  6.5 0.0 all-gather.5.cloned.1.call-start
  6.5 0.7 all-gather.5.cloned.1.call-update
  7.3 0.0 all-gather.7.cloned.1.call-start
  7.3 0.7 all-gather.7.cloned.1.call-update
  8.0 0.0 all-gather.9.cloned.1.call-start
  8.1 0.7 all-gather.9.cloned.1.call-update
  8.7 22.0 %all-gather = s32[16,1,2]{2,1,0:T(1,128)S(1)} all-gather(s32[1,1,2]{2,1,0:T(1,128)} %bitcast.173), channel_id=1, replica_groups=mesh['row'=8,'col'=16] {'col'}, dimensions={0}, use_global_device_ids=true | all-gather | bytes 136 | tf_op jit(solution)/shard_map/all_gather | solution.py:55
  30.7 0.1 copy.35
  30.8 1.2 dynamic-slice
  32.7 31.0 %all-gather.5.cloned.1.call-done = bf16[2,16,4,128,128]{4,3,2,1,0:T(8,128)(2,1)} async-done(((bf16[2,1,4,128,128]{4,3,2,1,0:T(8,128)(2,1)}), bf16[2,16,4,128,128]{4,3,2,1,0:T(8,128)(2,1)}) %all-gather.5.cloned.1.call-update) | async-done | bytes 4194320 | tf_op jit(solution)/shard_map/all_gather | solution.py:54
  63.7 4.6 %broadcast_multiply_fusion = bf16[2,16,4,128,128]{4,3,2,1,0:T(8,128)(2,1)} fusion(bf16[2,16,4,128,128]{4,3,2,1,0:T(8,128)(2,1)} %all-gather.5.cloned.1.call-done, bf16[2,16]{1,0:T(2,128)(2,1)S(1)} %convert_bitcast_fusion.1), kind=kLoop, calls=%fused_computation.5 | loop fusion | flops 2097152 | bytes 8388672 | tf_op jit(solution)/shard_map/mul | solution.py:57
  68.3 33.3 %all-gather.7.cloned.1.call-done = bf16[16,1,10,128,128]{4,3,2,1,0:T(8,128)(2,1)} async-done(((bf16[2,1,10,128,128]{4,3,2,1,0:T(8,128)(2,1)}), bf16[16,1,10,128,128]{4,3,2,1,0:T(8,128)(2,1)}) %all-gather.7.cloned.1.call-update) | async-done | bytes 5242896 | tf_op jit(solution)/shard_map/all_gather | solution.py:50
  101.6 7.8 %copy.36 = bf16[16,1,10,128,128]{3,4,2,0,1:T(8,128)(2,1)} copy(bf16[16,1,10,128,128]{4,3,2,1,0:T(8,128)(2,1)} %all-gather.7.cloned.1.call-done) | data formatting | bytes 10485760 | tf_op jit(solution)/shard_map/all_gather | solution.py:50
  109.4 9.0 %bitcast_convert_fusion = bf16[2,512,1280]{2,1,0:T(8,128)(2,1)S(1)} fusion(bf16[2,16,512,128]{3,2,1,0:T(8,128)(2,1)} %bitcast.167, bf16[16,128,1280,1]{1,2,0,3:T(8,128)(2,1)} %bitcast.166), kind=kOutput, calls=%fused_computation.2 | convolution fusion | flops 5370019840 | bytes 12058624 | tf_op jit(solution)/shard_map/cnmv,nvz->cmz/dot_general | solution.py:59
  118.3 3.2 %reshape.36 = bf16[2,4,128,10,128]{4,3,2,1,0:T(8,128)(2,1)} reshape(bf16[2,512,1280]{2,1,0:T(8,128)(2,1)S(1)} %bitcast_convert_fusion) | data formatting | bytes 5242880 | tf_op jit(solution)/shard_map/reshape | solution.py:60
  121.5 62.8 %all-gather.9.cloned.1.call-done = bf16[2,16,10,128,128]{4,3,2,0,1:T(8,128)(2,1)} async-done(((bf16[2,1,10,128,128]{4,3,2,0,1:T(8,128)(2,1)}), bf16[2,16,10,128,128]{4,3,2,0,1:T(8,128)(2,1)}) %all-gather.9.cloned.1.call-update) | async-done | bytes 10485776 | tf_op jit(solution)/shard_map/all_gather | solution.py:63
  184.3 10.9 %fusion.3 = f32[16,4,128,128]{2,3,0,1:T(8,128)} fusion(bf16[2,16,10,128,128]{4,3,2,0,1:T(8,128)(2,1)} %all-gather.9.cloned.1.call-done, bf16[2,4,128,10,128,1]{4,3,2,1,0,5:T(8,128)(2,1)} %bitcast.168), kind=kOutput, calls=%fused_computation.4 | convolution fusion | flops 5368709120 | bytes 17301504 | tf_op jit(solution)/shard_map/caqux,cpuqy->apxy/dot_general | solution.py:65
  195.2 58.5 %all-reduce.2 = bf16[16,4,128,128]{2,3,0,1:T(8,128)(2,1)S(1)} all-reduce(f32[16,4,128,128]{2,3,0,1:T(8,128)} %fusion.3), channel_id=2, replica_groups=mesh['row'=8,'col'=16] {'row'}, use_global_device_ids=true, to_apply=%region_0.0.clone | all-reduce | flops 1048576 | bytes 6291456
  253.7 0.2 copy.41
  253.9 1.5 collective-permute-start
  255.4 3.5 %collective-permute-done = bf16[4,128,128]{2,1,0:T(8,128)(2,1)S(1)} collective-permute-done((bf16[4,128,128]{2,1,0:T(8,128)(2,1)S(1)}, bf16[4,128,128]{2,1,0:T(8,128)(2,1)S(1)}, u32[]{:S(2)}, u32[]{:S(2)}) %collective-permute-start) | collective-permute-done | bytes 131104 | tf_op jit(solution)/shard_map/ppermute | solution.py:11
  259.0 0.1 fusion.42
  259.1 0.1 collective-permute-start.1
  259.2 1.3 collective-permute-done.1
  260.5 0.1 select_bitcast_fusion.14
  260.6 0.1 fusion.38
  260.6 3.0 collective-permute-start.2
  263.7 4.1 %collective-permute-done.2 = bf16[4,128,128]{2,1,0:T(8,128)(2,1)S(1)} collective-permute-done((bf16[4,128,128]{2,1,0:T(8,128)(2,1)S(1)}, bf16[4,128,128]{2,1,0:T(8,128)(2,1)S(1)}, u32[]{:S(2)}, u32[]{:S(2)}) %collective-permute-start.2) | collective-permute-done | bytes 131104 | tf_op jit(solution)/shard_map/ppermute | solution.py:11
  267.8 0.1 select_bitcast_fusion.12
  267.8 0.1 fusion.34
  267.9 0.1 collective-permute-start.3
  268.0 1.3 collective-permute-done.3
  269.3 0.1 select_bitcast_fusion.10
  269.4 0.1 fusion.30
  269.5 0.1 collective-permute-start.4
  269.6 5.5 %collective-permute-done.4 = bf16[4,128,128]{2,1,0:T(8,128)(2,1)S(1)} collective-permute-done((bf16[4,128,128]{2,1,0:T(8,128)(2,1)S(1)}, bf16[4,128,128]{2,1,0:T(8,128)(2,1)S(1)}, u32[]{:S(2)}, u32[]{:S(2)}) %collective-permute-start.4) | collective-permute-done | bytes 131104 | tf_op jit(solution)/shard_map/ppermute | solution.py:11
  275.1 0.1 select_bitcast_fusion.8
  275.2 0.1 fusion.26
  275.3 1.4 collective-permute-start.5
  276.6 3.7 %collective-permute-done.5 = bf16[4,128,128]{2,1,0:T(8,128)(2,1)S(1)} collective-permute-done((bf16[4,128,128]{2,1,0:T(8,128)(2,1)S(1)}, bf16[4,128,128]{2,1,0:T(8,128)(2,1)S(1)}, u32[]{:S(2)}, u32[]{:S(2)}) %collective-permute-start.5) | collective-permute-done | bytes 131104 | tf_op jit(solution)/shard_map/ppermute | solution.py:11
  280.3 0.1 select_bitcast_fusion.6
  280.4 0.1 fusion.22
  280.4 0.4 collective-permute-start.6
  280.9 5.7 %collective-permute-done.6 = bf16[4,128,128]{2,1,0:T(8,128)(2,1)S(1)} collective-permute-done((bf16[4,128,128]{2,1,0:T(8,128)(2,1)S(1)}, bf16[4,128,128]{2,1,0:T(8,128)(2,1)S(1)}, u32[]{:S(2)}, u32[]{:S(2)}) %collective-permute-start.6) | collective-permute-done | bytes 131104 | tf_op jit(solution)/shard_map/ppermute | solution.py:11
  286.6 0.1 select_bitcast_fusion.4
  286.6 0.1 fusion.18
  286.7 0.1 collective-permute-start.7
  286.8 6.4 %collective-permute-done.7 = bf16[4,128,128]{2,1,0:T(8,128)(2,1)S(1)} collective-permute-done((bf16[4,128,128]{2,1,0:T(8,128)(2,1)S(1)}, bf16[4,128,128]{2,1,0:T(8,128)(2,1)S(1)}, u32[]{:S(2)}, u32[]{:S(2)}) %collective-permute-start.7) | collective-permute-done | bytes 131104 | tf_op jit(solution)/shard_map/ppermute | solution.py:11
  293.2 0.1 select_bitcast_fusion.2
  293.3 0.1 fusion.14
  293.4 3.0 collective-permute-start.8
  296.4 3.6 %collective-permute-done.8 = bf16[4,128,128]{2,1,0:T(8,128)(2,1)S(1)} collective-permute-done((bf16[4,128,128]{2,1,0:T(8,128)(2,1)S(1)}, bf16[4,128,128]{2,1,0:T(8,128)(2,1)S(1)}, u32[]{:S(2)}, u32[]{:S(2)}) %collective-permute-start.8) | collective-permute-done | bytes 131104 | tf_op jit(solution)/shard_map/ppermute | solution.py:11
  299.9 0.1 select_bitcast_fusion
  300.0 0.1 fusion.10
  300.1 0.1 collective-permute-start.9
  300.2 6.5 %collective-permute-done.9 = bf16[4,128,128]{2,1,0:T(8,128)(2,1)S(1)} collective-permute-done((bf16[4,128,128]{2,1,0:T(8,128)(2,1)S(1)}, bf16[4,128,128]{2,1,0:T(8,128)(2,1)S(1)}, u32[]{:S(2)}, u32[]{:S(2)}) %collective-permute-start.9) | collective-permute-done | bytes 131104 | tf_op jit(solution)/shard_map/ppermute | solution.py:11
  306.6 0.1 broadcast_select_fusion.1
  306.7 0.2 copy.42
  306.9 0.8 fusion.8
  (5 shorter events, 0.1 us)
Async XLA Ops:
  6.5 57.2 %all-gather.5.cloned.1.call-start = ((), (), s32[]{:S(2)}) async-start(), calls=%async_computation | async-start | bytes 4456448 | tf_op jit(solution)/shard_map/all_gather | solution.py:54
  7.3 94.3 %all-gather.7.cloned.1.call-start = ((), (), s32[]{:S(2)}) async-start(), calls=%async_computation.1 | async-start | bytes 5898240 | tf_op jit(solution)/shard_map/all_gather | solution.py:50
  8.0 176.3 %all-gather.9.cloned.1.call-start = ((), (), s32[]{:S(2)}) async-start(), calls=%async_computation.2 | async-start | bytes 11141120 | tf_op jit(solution)/shard_map/all_gather | solution.py:63
  253.9 5.0 %collective-permute-start = (bf16[4,128,128]{2,1,0:T(8,128)(2,1)S(1)}, bf16[4,128,128]{2,1,0:T(8,128)(2,1)S(1)}, u32[]{:S(2)}, u32[]{:S(2)}) collective-permute-start(bf16[4,128,128]{2,1,0:T(8,128)(2,1)S(1)} %dynamic-slice_bitcast_fusion), channel_id=1, source_target_pairs={{0,1},{1,0},{2,3},{3,2},{4,5},{5,4},{6,7},{7,6},{8,9},{9,8},{10,11... | collective-permute-start | bytes 393224 | tf_op jit(solution)/shard_map/ppermute | solution.py:11
  259.1 1.4 collective-permute-start.1
  260.6 7.1 %collective-permute-start.2 = (bf16[4,128,128]{2,1,0:T(8,128)(2,1)S(1)}, bf16[4,128,128]{2,1,0:T(8,128)(2,1)S(1)}, u32[]{:S(2)}, u32[]{:S(2)}) collective-permute-start(bf16[4,128,128]{2,1,0:T(8,128)(2,1)S(1)} %fusion.38), channel_id=1, source_target_pairs={{0,2},{1,3},{2,0},{3,1},{4,6},{5,7},{6,4},{7,5},{8,10},{9,11},{10,... | collective-permute-start | bytes 393224 | tf_op jit(solution)/shard_map/ppermute | solution.py:11
  267.9 1.4 collective-permute-start.3
  269.5 5.6 %collective-permute-start.4 = (bf16[4,128,128]{2,1,0:T(8,128)(2,1)S(1)}, bf16[4,128,128]{2,1,0:T(8,128)(2,1)S(1)}, u32[]{:S(2)}, u32[]{:S(2)}) collective-permute-start(bf16[4,128,128]{2,1,0:T(8,128)(2,1)S(1)} %fusion.30), channel_id=1, source_target_pairs={{0,32},{16,48},{32,0},{48,16},{64,96},{80,112},{96,64},{112,80},{1... | collective-permute-start | bytes 393224 | tf_op jit(solution)/shard_map/ppermute | solution.py:11
  275.3 5.0 %collective-permute-start.5 = (bf16[4,128,128]{2,1,0:T(8,128)(2,1)S(1)}, bf16[4,128,128]{2,1,0:T(8,128)(2,1)S(1)}, u32[]{:S(2)}, u32[]{:S(2)}) collective-permute-start(bf16[4,128,128]{2,1,0:T(8,128)(2,1)S(1)} %fusion.26), channel_id=1, source_target_pairs={{0,4},{1,5},{2,6},{3,7},{4,0},{5,1},{6,2},{7,3},{8,12},{9,13},{10,... | collective-permute-start | bytes 393224 | tf_op jit(solution)/shard_map/ppermute | solution.py:11
  280.4 6.1 %collective-permute-start.6 = (bf16[4,128,128]{2,1,0:T(8,128)(2,1)S(1)}, bf16[4,128,128]{2,1,0:T(8,128)(2,1)S(1)}, u32[]{:S(2)}, u32[]{:S(2)}) collective-permute-start(bf16[4,128,128]{2,1,0:T(8,128)(2,1)S(1)} %fusion.22), channel_id=1, source_target_pairs={{0,32},{16,48},{32,0},{48,16},{64,96},{80,112},{96,64},{112,80},{1... | collective-permute-start | bytes 393224 | tf_op jit(solution)/shard_map/ppermute | solution.py:11
  286.7 6.6 %collective-permute-start.7 = (bf16[4,128,128]{2,1,0:T(8,128)(2,1)S(1)}, bf16[4,128,128]{2,1,0:T(8,128)(2,1)S(1)}, u32[]{:S(2)}, u32[]{:S(2)}) collective-permute-start(bf16[4,128,128]{2,1,0:T(8,128)(2,1)S(1)} %fusion.18), channel_id=1, source_target_pairs={{0,64},{16,80},{32,96},{48,112},{64,0},{80,16},{96,32},{112,48},{1... | collective-permute-start | bytes 393224 | tf_op jit(solution)/shard_map/ppermute | solution.py:11
  293.4 6.6 %collective-permute-start.8 = (bf16[4,128,128]{2,1,0:T(8,128)(2,1)S(1)}, bf16[4,128,128]{2,1,0:T(8,128)(2,1)S(1)}, u32[]{:S(2)}, u32[]{:S(2)}) collective-permute-start(bf16[4,128,128]{2,1,0:T(8,128)(2,1)S(1)} %fusion.14), channel_id=1, source_target_pairs={{0,8},{1,9},{2,10},{3,11},{4,12},{5,13},{6,14},{7,15},{8,0},{9,1},... | collective-permute-start | bytes 393224 | tf_op jit(solution)/shard_map/ppermute | solution.py:11
  300.1 6.6 %collective-permute-start.9 = (bf16[4,128,128]{2,1,0:T(8,128)(2,1)S(1)}, bf16[4,128,128]{2,1,0:T(8,128)(2,1)S(1)}, u32[]{:S(2)}, u32[]{:S(2)}) collective-permute-start(bf16[4,128,128]{2,1,0:T(8,128)(2,1)S(1)} %fusion.10), channel_id=1, source_target_pairs={{0,64},{16,80},{32,96},{48,112},{64,0},{80,16},{96,32},{112,48},{1... | collective-permute-start | bytes 393224 | tf_op jit(solution)/shard_map/ppermute | solution.py:11
Sparse Core Ops, SparseCore 0:
  9.5 54.1 all-gather.4
  65.4 36.0 all-gather.6
  103.7 80.5 all-gather.8
where the time goes:
time: 315 us; the launch traced here: 314 us
  waiting for transfers between devices  171 us (54%)
  blocking collectives  80.5 us (26%)
  matrix products  19.9 us (6%)
  between operations  14 us (4%)
  local copies, waits for them, and re-layouts  12.7 us (4%)
  starting transfers between devices  9.81 us (3%)
  other arithmetic  6.55 us (2%)
    all_gather x1, waiting for transfers between devices, body(): spread = lax.all_gather(cholesky, 'col', axis=1, tiled=True)  62.8 us
    unnamed x1, blocking collectives  58.5 us
    ppermute x10, waiting for transfers between devices, from_partner(): return lax.ppermute(value, axis, pairs)  41.7 us
    all_gather x1, waiting for transfers between devices, body(): column = lax.all_gather(cholesky, 'row', axis=0, tiled=True)  33.3 us
    all_gather x1, waiting for transfers between devices, body(): amp_block = lax.all_gather(amplitudes, 'col', axis=1, tiled=True)  31 us
    all_gather x1, blocking collectives, body(): mask_block = lax.all_gather(tile_mask, 'col', axis=1, tiled=True)  22 us
    dot_general x1, matrix products, body(): jnp.einsum('caqux,cpuqy->apxy', spread, halves, preferred_element_type=jn...  10.9 us
    ppermute x10, starting transfers between devices, from_partner(): return lax.ppermute(value, axis, pairs)  9.73 us
  transfers between devices with their start and end apart: 13, of which 13 were waited for; matrix products, arithmetic and copies ran while one was open for 8% of the time, Pallas kernels for 0%

commit v1 on v0

--- a/solution.py
+++ b/solution.py
@@ -51,7 +51,9 @@
     column_mats = jnp.transpose(column[:, 0], (0, 2, 1, 3)).reshape(
         column.shape[0], tile_edge, vectors * tile_edge
     )
-    amp_block = lax.all_gather(amplitudes, "col", axis=1, tiled=True)
+    amp_block = jnp.concatenate(
+        lax.all_to_all(jnp.stack([amplitudes] * lax.axis_size("col")), "col", 0, 0), axis=1
+    )
     mask_block = lax.all_gather(tile_mask, "col", axis=1, tiled=True)
     tile_count = amp_block.shape[1]
     masked = amp_block * mask_block.astype(jnp.bfloat16)[:, :, None, None, None]

time: 315 us -> 272 us (0.86)
  waiting for transfers between devices: 171 us -> 55.1 us
  blocking collectives: 80.5 us -> 141 us
  starting transfers between devices: 9.81 us -> 17.8 us
  local copies, waits for them, and re-layouts: 12.7 us -> 16.2 us
    all_gather x1, blocking collectives: 22 us -> 82.6 us  [body(): mask_block = lax.all_gather(tile_mask, 'col', axis=1, tiled=True)]
    all_gather x1, waiting for transfers between devices: 62.8 us -> 11.9 us  [body(): spread = lax.all_gather(cholesky, 'col', axis=1, tiled=True)]
    all_gather x1, waiting for transfers between devices: 33.3 us -> 0.01 us  [body(): column = lax.all_gather(cholesky, 'row', axis=0, tiled=True)]
    all_gather x1 -> x0, waiting for transfers between devices: 31 us -> none  [body(): amp_block = lax.all_gather(amplitudes, 'col', axis=1, tiled=True)]
    all_to_all x0 -> x1, starting transfers between devices: none -> 8.14 us  [body(): lax.all_to_all(jnp.stack([amplitudes] * lax.axis_size('col')), 'col', 0, 0)]
    another operation x0 -> x1, local copies, waits for them, and re-layouts: none -> 3.98 us  [body(): jnp.stack([amplitudes] * lax.axis_size('col'))]
  transfers between devices with their start and end apart: 13 -> 13, of which waited for: 13 -> 11; matrix products, arithmetic and copies ran while one was open for 8% -> 11% of each run, Pallas kernels for 0% -> 0%
where the time goes in v1:
time: 272 us; the launch traced here: 271 us
  blocking collectives  141 us (52%)
  waiting for transfers between devices  55.1 us (20%)
  matrix products  20 us (7%)
  starting transfers between devices  17.8 us (7%)
  local copies, waits for them, and re-layouts  16.2 us (6%)
  between operations  14.3 us (5%)
  other arithmetic  6.55 us (2%)
    all_gather x1, blocking collectives, body(): mask_block = lax.all_gather(tile_mask, 'col', axis=1, tiled=True)  82.6 us
    unnamed x1, blocking collectives  58.5 us
    ppermute x10, waiting for transfers between devices, from_partner(): return lax.ppermute(value, axis, pairs)  41.8 us
    all_gather x1, waiting for transfers between devices, body(): spread = lax.all_gather(cholesky, 'col', axis=1, tiled=True)  11.9 us
    dot_general x1, matrix products, body(): jnp.einsum('caqux,cpuqy->apxy', spread, halves, preferred_element_type=jn...  10.9 us
    ppermute x10, starting transfers between devices, from_partner(): return lax.ppermute(value, axis, pairs)  9.64 us
    dot_general x1, matrix products, body(): jnp.einsum('cnmv,nvz->cmz', masked, column_mats, preferred_element_type=j...  9.16 us
    all_to_all x1, starting transfers between devices, body(): lax.all_to_all(jnp.stack([amplitudes] * lax.axis_size('col')), 'col', 0, 0)  8.14 us
  transfers between devices with their start and end apart: 13, of which 11 were waited for; matrix products, arithmetic and copies ran while one was open for 11% of the time, Pallas kernels for 0%

profile of v1, /device:TPU:0, one launch (start us, length us, event | category | flops | bytes accessed | tf_op | source)
XLA Modules:
  0.0 271.1 jit_solution(1501245401231915488)
XLA Ops:
  6.5 0.0 all-gather.4.cloned.1.call-start
  6.5 0.7 all-gather.4.cloned.1.call-update
  7.3 0.0 all-gather.6.cloned.1.call-start
  7.3 0.7 all-gather.6.cloned.1.call-update
  8.0 4.0 %stack.109 = bf16[16,2,1,4,128,128]{5,4,3,1,2,0:T(8,128)(2,1)} broadcast(bf16[2,4,128,128]{3,2,1,0:T(8,128)(2,1)} %bitcast.177), dimensions={1,3,4,5} | broadcast | bytes 4456448 | tf_op jit(solution)/shard_map/stack | solution.py:55
  12.0 0.0 copy-start
  12.0 0.0 copy-start.1
  12.0 8.1 %all-to-all-start = ((bf16[16,2,1,4,128,128]{5,4,3,1,2,0:T(8,128)(2,1)}), bf16[16,2,1,4,128,128]{5,4,3,1,2,0:T(8,128)(2,1)}, u32[]{:S(2)}, u32[]{:S(2)}) async-start(bf16[16,2,1,4,128,128]{5,4,3,1,2,0:T(8,128)(2,1)} %stack.109), calls=%async_computation | async-start | bytes 8388608 | tf_op jit(solution)/shard_map/all_to_all | solution.py:55
  20.1 0.0 copy-done
  20.2 82.6 %all-gather = s32[16,1,2]{2,1,0:T(1,128)S(1)} all-gather(s32[1,1,2]{2,1,0:T(1,128)S(1)} %bitcast.178), channel_id=1, replica_groups=mesh['row'=8,'col'=16] {'col'}, dimensions={0}, use_global_device_ids=true | all-gather | bytes 136 | tf_op jit(solution)/shard_map/all_gather | solution.py:57
  102.8 0.1 copy.38
  102.8 0.1 copy.39
  102.9 0.0 copy-done.1
  103.0 0.6 dynamic-slice
  104.2 0.0 all-to-all-done
  104.2 4.5 %bitcast_multiply_fusion = bf16[2,16,1,4,128,128]{5,4,3,0,2,1:T(8,128)(2,1)} fusion(bf16[16,2,1,4,128,128]{5,4,3,1,2,0:T(8,128)(2,1)} %all-to-all-done, bf16[2,16]{0,1:T(8,128)(2,1)S(1)} %copy.39), kind=kLoop, calls=%fused_computation.3 | loop fusion | flops 2097152 | bytes 8388672 | tf_op jit(solution)/shard_map/mul | solution.py:59
  108.8 0.0 all-gather.4.cloned.1.call-done
  108.8 7.9 %copy.40 = bf16[16,1,10,128,128]{3,4,2,0,1:T(8,128)(2,1)} copy(bf16[16,1,10,128,128]{4,3,2,1,0:T(8,128)(2,1)} %all-gather.4.cloned.1.call-done) | data formatting | bytes 10485760 | tf_op jit(solution)/shard_map/all_gather | solution.py:50
  116.6 9.2 %bitcast_convert_fusion = bf16[2,512,1280]{2,1,0:T(8,128)(2,1)S(1)} fusion(bf16[2,16,512,128]{3,2,0,1:T(8,128)(2,1)} %bitcast.171, bf16[16,128,1280,1]{1,2,3,0:T(8,128)(2,1)} %bitcast.170), kind=kOutput, calls=%fused_computation.2 | convolution fusion | flops 5370019840 | bytes 12058624 | tf_op jit(solution)/shard_map/cnmv,nvz->cmz/dot_general | solution.py:61
  125.8 3.2 %reshape.44 = bf16[2,4,128,10,128]{4,3,2,1,0:T(8,128)(2,1)} reshape(bf16[2,512,1280]{2,1,0:T(8,128)(2,1)S(1)} %bitcast_convert_fusion) | data formatting | bytes 5242880 | tf_op jit(solution)/shard_map/reshape | solution.py:62
  129.0 11.9 %all-gather.6.cloned.1.call-done = bf16[2,16,10,128,128]{4,3,2,0,1:T(8,128)(2,1)} async-done(((bf16[2,1,10,128,128]{4,3,2,0,1:T(8,128)(2,1)}), bf16[2,16,10,128,128]{4,3,2,0,1:T(8,128)(2,1)}) %all-gather.6.cloned.1.call-update) | async-done | bytes 10485776 | tf_op jit(solution)/shard_map/all_gather | solution.py:65
  140.9 10.9 %fusion.3 = f32[16,4,128,128]{2,3,0,1:T(8,128)} fusion(bf16[2,16,10,128,128]{4,3,2,0,1:T(8,128)(2,1)} %all-gather.6.cloned.1.call-done, bf16[2,4,128,10,128,1]{4,3,2,1,0,5:T(8,128)(2,1)} %bitcast.172), kind=kOutput, calls=%fused_computation.5 | convolution fusion | flops 5368709120 | bytes 17301504 | tf_op jit(solution)/shard_map/caqux,cpuqy->apxy/dot_general | solution.py:67
  151.8 58.5 %all-reduce.2 = bf16[16,4,128,128]{2,3,0,1:T(8,128)(2,1)S(1)} all-reduce(f32[16,4,128,128]{2,3,0,1:T(8,128)} %fusion.3), channel_id=2, replica_groups=mesh['row'=8,'col'=16] {'row'}, use_global_device_ids=true, to_apply=%region_0.0.clone | all-reduce | flops 1048576 | bytes 6291456
  210.3 0.2 copy.45
  210.5 1.5 collective-permute-start
  212.1 3.5 %collective-permute-done = bf16[4,128,128]{2,1,0:T(8,128)(2,1)S(1)} collective-permute-done((bf16[4,128,128]{2,1,0:T(8,128)(2,1)S(1)}, bf16[4,128,128]{2,1,0:T(8,128)(2,1)S(1)}, u32[]{:S(2)}, u32[]{:S(2)}) %collective-permute-start) | collective-permute-done | bytes 131104 | tf_op jit(solution)/shard_map/ppermute | solution.py:11
  215.6 0.1 fusion.42
  215.7 0.1 collective-permute-start.1
  215.8 1.3 collective-permute-done.1
  217.1 0.1 select_bitcast_fusion.14
  217.2 0.1 fusion.38
  217.2 3.0 %collective-permute-start.2 = (bf16[4,128,128]{2,1,0:T(8,128)(2,1)S(1)}, bf16[4,128,128]{2,1,0:T(8,128)(2,1)S(1)}, u32[]{:S(2)}, u32[]{:S(2)}) collective-permute-start(bf16[4,128,128]{2,1,0:T(8,128)(2,1)S(1)} %fusion.38), channel_id=1, source_target_pairs={{0,2},{1,3},{2,0},{3,1},{4,6},{5,7},{6,4},{7,5},{8,10},{9,11},{10,... | collective-permute-start | bytes 393224 | tf_op jit(solution)/shard_map/ppermute | solution.py:11
  220.2 4.1 %collective-permute-done.2 = bf16[4,128,128]{2,1,0:T(8,128)(2,1)S(1)} collective-permute-done((bf16[4,128,128]{2,1,0:T(8,128)(2,1)S(1)}, bf16[4,128,128]{2,1,0:T(8,128)(2,1)S(1)}, u32[]{:S(2)}, u32[]{:S(2)}) %collective-permute-start.2) | collective-permute-done | bytes 131104 | tf_op jit(solution)/shard_map/ppermute | solution.py:11
  224.4 0.1 select_bitcast_fusion.12
  224.4 0.1 fusion.34
  224.5 0.1 collective-permute-start.3
  224.6 1.3 collective-permute-done.3
  225.9 0.1 select_bitcast_fusion.10
  226.0 0.1 fusion.30
  226.1 0.1 collective-permute-start.4
  226.2 5.5 %collective-permute-done.4 = bf16[4,128,128]{2,1,0:T(8,128)(2,1)S(1)} collective-permute-done((bf16[4,128,128]{2,1,0:T(8,128)(2,1)S(1)}, bf16[4,128,128]{2,1,0:T(8,128)(2,1)S(1)}, u32[]{:S(2)}, u32[]{:S(2)}) %collective-permute-start.4) | collective-permute-done | bytes 131104 | tf_op jit(solution)/shard_map/ppermute | solution.py:11
  231.7 0.1 select_bitcast_fusion.8
  231.8 0.1 fusion.26
  231.8 1.3 collective-permute-start.5
  233.2 3.7 %collective-permute-done.5 = bf16[4,128,128]{2,1,0:T(8,128)(2,1)S(1)} collective-permute-done((bf16[4,128,128]{2,1,0:T(8,128)(2,1)S(1)}, bf16[4,128,128]{2,1,0:T(8,128)(2,1)S(1)}, u32[]{:S(2)}, u32[]{:S(2)}) %collective-permute-start.5) | collective-permute-done | bytes 131104 | tf_op jit(solution)/shard_map/ppermute | solution.py:11
  236.9 0.1 select_bitcast_fusion.6
  237.0 0.1 fusion.22
  237.0 0.4 collective-permute-start.6
  237.5 5.7 %collective-permute-done.6 = bf16[4,128,128]{2,1,0:T(8,128)(2,1)S(1)} collective-permute-done((bf16[4,128,128]{2,1,0:T(8,128)(2,1)S(1)}, bf16[4,128,128]{2,1,0:T(8,128)(2,1)S(1)}, u32[]{:S(2)}, u32[]{:S(2)}) %collective-permute-start.6) | collective-permute-done | bytes 131104 | tf_op jit(solution)/shard_map/ppermute | solution.py:11
  243.1 0.1 select_bitcast_fusion.4
  243.2 0.1 fusion.18
  243.3 0.1 collective-permute-start.7
  243.4 6.4 %collective-permute-done.7 = bf16[4,128,128]{2,1,0:T(8,128)(2,1)S(1)} collective-permute-done((bf16[4,128,128]{2,1,0:T(8,128)(2,1)S(1)}, bf16[4,128,128]{2,1,0:T(8,128)(2,1)S(1)}, u32[]{:S(2)}, u32[]{:S(2)}) %collective-permute-start.7) | collective-permute-done | bytes 131104 | tf_op jit(solution)/shard_map/ppermute | solution.py:11
  249.8 0.1 select_bitcast_fusion.2
  249.9 0.1 fusion.14
  250.0 2.9 %collective-permute-start.8 = (bf16[4,128,128]{2,1,0:T(8,128)(2,1)S(1)}, bf16[4,128,128]{2,1,0:T(8,128)(2,1)S(1)}, u32[]{:S(2)}, u32[]{:S(2)}) collective-permute-start(bf16[4,128,128]{2,1,0:T(8,128)(2,1)S(1)} %fusion.14), channel_id=1, source_target_pairs={{0,8},{1,9},{2,10},{3,11},{4,12},{5,13},{6,14},{7,15},{8,0},{9,1},... | collective-permute-start | bytes 393224 | tf_op jit(solution)/shard_map/ppermute | solution.py:11
  252.9 3.6 %collective-permute-done.8 = bf16[4,128,128]{2,1,0:T(8,128)(2,1)S(1)} collective-permute-done((bf16[4,128,128]{2,1,0:T(8,128)(2,1)S(1)}, bf16[4,128,128]{2,1,0:T(8,128)(2,1)S(1)}, u32[]{:S(2)}, u32[]{:S(2)}) %collective-permute-start.8) | collective-permute-done | bytes 131104 | tf_op jit(solution)/shard_map/ppermute | solution.py:11
  256.5 0.1 select_bitcast_fusion
  256.6 0.1 fusion.10
  256.7 0.1 collective-permute-start.9
  256.8 6.5 %collective-permute-done.9 = bf16[4,128,128]{2,1,0:T(8,128)(2,1)S(1)} collective-permute-done((bf16[4,128,128]{2,1,0:T(8,128)(2,1)S(1)}, bf16[4,128,128]{2,1,0:T(8,128)(2,1)S(1)}, u32[]{:S(2)}, u32[]{:S(2)}) %collective-permute-start.9) | collective-permute-done | bytes 131104 | tf_op jit(solution)/shard_map/ppermute | solution.py:11
  263.2 0.1 broadcast_select_fusion.1
  263.3 0.2 copy.46
  263.5 0.8 fusion.8
  (5 shorter events, 0.1 us)
Async XLA Ops:
  6.5 102.2 %all-gather.4.cloned.1.call-start = ((), (), s32[]{:S(2)}) async-start(), calls=%async_computation.1 | async-start | bytes 5898240 | tf_op jit(solution)/shard_map/all_gather | solution.py:50
  7.3 133.6 %all-gather.6.cloned.1.call-start = ((), (), s32[]{:S(2)}) async-start(), calls=%async_computation.2 | async-start | bytes 11141120 | tf_op jit(solution)/shard_map/all_gather | solution.py:65
  12.0 8.2 %copy-start = (s32[2,1]{0,1:T(1,128)S(1)}, s32[2,1]{0,1:T(1,128)}, u32[]{:S(2)}) copy-start(s32[2,1]{0,1:T(1,128)} %param.5) | copy-start | bytes 28
  12.0 91.0 %copy-start.1 = (u32[128]{0:T(128)S(1)}, u32[128]{0:T(128)}, u32[]{:S(2)}) copy-start(u32[128]{0:T(128)} %constant.71) | copy-start | bytes 1540
  12.0 92.2 %all-to-all-start = ((bf16[16,2,1,4,128,128]{5,4,3,1,2,0:T(8,128)(2,1)}), bf16[16,2,1,4,128,128]{5,4,3,1,2,0:T(8,128)(2,1)}, u32[]{:S(2)}, u32[]{:S(2)}) async-start(bf16[16,2,1,4,128,128]{5,4,3,1,2,0:T(8,128)(2,1)} %stack.109), calls=%async_computation | async-start | bytes 8388608 | tf_op jit(solution)/shard_map/all_to_all | solution.py:55
  210.5 5.0 %collective-permute-start = (bf16[4,128,128]{2,1,0:T(8,128)(2,1)S(1)}, bf16[4,128,128]{2,1,0:T(8,128)(2,1)S(1)}, u32[]{:S(2)}, u32[]{:S(2)}) collective-permute-start(bf16[4,128,128]{2,1,0:T(8,128)(2,1)S(1)} %dynamic-slice_bitcast_fusion), channel_id=1, source_target_pairs={{0,1},{1,0},{2,3},{3,2},{4,5},{5,4},{6,7},{7,6},{8,9},{9,8},{10,11... | collective-permute-start | bytes 393224 | tf_op jit(solution)/shard_map/ppermute | solution.py:11
  215.7 1.4 collective-permute-start.1
  217.2 7.1 %collective-permute-start.2 = (bf16[4,128,128]{2,1,0:T(8,128)(2,1)S(1)}, bf16[4,128,128]{2,1,0:T(8,128)(2,1)S(1)}, u32[]{:S(2)}, u32[]{:S(2)}) collective-permute-start(bf16[4,128,128]{2,1,0:T(8,128)(2,1)S(1)} %fusion.38), channel_id=1, source_target_pairs={{0,2},{1,3},{2,0},{3,1},{4,6},{5,7},{6,4},{7,5},{8,10},{9,11},{10,... | collective-permute-start | bytes 393224 | tf_op jit(solution)/shard_map/ppermute | solution.py:11
  224.5 1.4 collective-permute-start.3
  226.1 5.6 %collective-permute-start.4 = (bf16[4,128,128]{2,1,0:T(8,128)(2,1)S(1)}, bf16[4,128,128]{2,1,0:T(8,128)(2,1)S(1)}, u32[]{:S(2)}, u32[]{:S(2)}) collective-permute-start(bf16[4,128,128]{2,1,0:T(8,128)(2,1)S(1)} %fusion.30), channel_id=1, source_target_pairs={{0,32},{16,48},{32,0},{48,16},{64,96},{80,112},{96,64},{112,80},{1... | collective-permute-start | bytes 393224 | tf_op jit(solution)/shard_map/ppermute | solution.py:11
  231.8 5.0 %collective-permute-start.5 = (bf16[4,128,128]{2,1,0:T(8,128)(2,1)S(1)}, bf16[4,128,128]{2,1,0:T(8,128)(2,1)S(1)}, u32[]{:S(2)}, u32[]{:S(2)}) collective-permute-start(bf16[4,128,128]{2,1,0:T(8,128)(2,1)S(1)} %fusion.26), channel_id=1, source_target_pairs={{0,4},{1,5},{2,6},{3,7},{4,0},{5,1},{6,2},{7,3},{8,12},{9,13},{10,... | collective-permute-start | bytes 393224 | tf_op jit(solution)/shard_map/ppermute | solution.py:11
  237.0 6.1 %collective-permute-start.6 = (bf16[4,128,128]{2,1,0:T(8,128)(2,1)S(1)}, bf16[4,128,128]{2,1,0:T(8,128)(2,1)S(1)}, u32[]{:S(2)}, u32[]{:S(2)}) collective-permute-start(bf16[4,128,128]{2,1,0:T(8,128)(2,1)S(1)} %fusion.22), channel_id=1, source_target_pairs={{0,32},{16,48},{32,0},{48,16},{64,96},{80,112},{96,64},{112,80},{1... | collective-permute-start | bytes 393224 | tf_op jit(solution)/shard_map/ppermute | solution.py:11
  243.3 6.6 %collective-permute-start.7 = (bf16[4,128,128]{2,1,0:T(8,128)(2,1)S(1)}, bf16[4,128,128]{2,1,0:T(8,128)(2,1)S(1)}, u32[]{:S(2)}, u32[]{:S(2)}) collective-permute-start(bf16[4,128,128]{2,1,0:T(8,128)(2,1)S(1)} %fusion.18), channel_id=1, source_target_pairs={{0,64},{16,80},{32,96},{48,112},{64,0},{80,16},{96,32},{112,48},{1... | collective-permute-start | bytes 393224 | tf_op jit(solution)/shard_map/ppermute | solution.py:11
  250.0 6.6 %collective-permute-start.8 = (bf16[4,128,128]{2,1,0:T(8,128)(2,1)S(1)}, bf16[4,128,128]{2,1,0:T(8,128)(2,1)S(1)}, u32[]{:S(2)}, u32[]{:S(2)}) collective-permute-start(bf16[4,128,128]{2,1,0:T(8,128)(2,1)S(1)} %fusion.14), channel_id=1, source_target_pairs={{0,8},{1,9},{2,10},{3,11},{4,12},{5,13},{6,14},{7,15},{8,0},{9,1},... | collective-permute-start | bytes 393224 | tf_op jit(solution)/shard_map/ppermute | solution.py:11
  256.7 6.6 %collective-permute-start.9 = (bf16[4,128,128]{2,1,0:T(8,128)(2,1)S(1)}, bf16[4,128,128]{2,1,0:T(8,128)(2,1)S(1)}, u32[]{:S(2)}, u32[]{:S(2)}) collective-permute-start(bf16[4,128,128]{2,1,0:T(8,128)(2,1)S(1)} %fusion.10), channel_id=1, source_target_pairs={{0,64},{16,80},{32,96},{48,112},{64,0},{80,16},{96,32},{112,48},{1... | collective-permute-start | bytes 393224 | tf_op jit(solution)/shard_map/ppermute | solution.py:11
Sparse Core Ops, SparseCore 0:
  9.0 38.9 all-gather.3
  50.2 90.6 all-gather.5
